TPU v7x, 512 devices: a whole 4x8x8 slice. The times are simulated.
512 devices in a mesh: pitch: 32 (over x, z), span: 8 (over y), row: 2 (over core).
Axes of the slice: x: 4, y: 8, z: 8, core: 2. Of those that a mesh axis runs over, the one named last changes fastest.
Arguments:
- fields: float32 [3, 512, 128, 512], P(None, 'pitch', 'span', 'row'), may hold values from -6 to 6
- diffusivity: float32 [512, 128, 512], P('pitch', 'span', 'row'), may hold values from 0.01 to 0.1
- mean_flow: bfloat16 [128, 2, 512], P('span', None, 'row'), may hold values from -6 to 6
- radial_kernel: bfloat16 [128, 128], replicated
- tracer_values: float32 [10, 1048576], P(None, ('pitch', 'span', 'row')), may hold values from -6 to 6
- tracer_cells: int32 [1048576], P(('pitch', 'span', 'row')), may hold values from 0 to 65535
- tracer_dest: int32 [1048576, 1], P(('pitch', 'span', 'row')), may hold values from 0 to 31; in each aligned block of 2048 rows (0 to 2047, 2048 to 4095, ...) at most 128 rows name the same one
- interface_map: int32 [2, 512], P('row', 'pitch'), may hold values from 0 to 511, as said below
Outputs:
- advected: float32 [3, 512, 128, 512], P(None, 'pitch', 'span', 'row')
- arrived: float32 [10, 2097152], P(None, ('pitch', 'span', 'row'))
Inputs may be any that keep to these rules, and one draw needn't show every extreme that they name: `tracer_cells`: the local index of the owning cell within the block of the device that holds the tracer, i * 16 * 256 + r * 256 + a for local indices i, r, a. `tracer_dest`: at most 128 of the tracers of one device go to one pitch index. `interface_map`: for one offset o of each draw, row 0 holds (i + o) mod 512 and row 1 holds (i - o) mod 512, so the two rows are inverse permutations.
All inputs are finite; a program needn't handle non-finite values.
Results may differ from a plain program's by a relative error of at most 0.0015.
Values may be sent and summed in bfloat16 or wider, within the bound.
A program may use at most 128 MiB of HBM per device.

v0:
```python
import jax
import jax.numpy as jnp
from jax import lax
from jax.sharding import PartitionSpec as P

SUB = 2
TIME_STEP = 0.9
AXIAL_SPEED = 0.15
PITCH_SPEED = 0.15


def swapped(block, axis, apart):
    count = lax.axis_size(axis)
    route = []
    for low in range(count):
        high = low | 1 << apart
        if high != low and high < count:
            route += [(low, high), (high, low)]
    return lax.ppermute(block, axis, route)


def padded(cells, sides, width):
    for axis, dim in sides:
        count = lax.axis_size(axis)
        head = lax.slice_in_dim(cells, 0, width, axis=dim)
        tail = lax.slice_in_dim(cells, cells.shape[dim] - width, cells.shape[dim], axis=dim)
        cells = jnp.concatenate(
            [
                lax.ppermute(tail, axis, [(i, (i + 1) % count) for i in range(count)]),
                cells,
                lax.ppermute(head, axis, [((i + 1) % count, i) for i in range(count)]),
            ],
            axis=dim,
        )
    return cells


def face_flux(left_values, right_values, left_kappa, right_kappa, face_speed):
    diffusion = -0.5 * (left_kappa + right_kappa) * (right_values - left_values)
    if face_speed is None:
        return diffusion
    return (
        jnp.maximum(face_speed, 0.0) * left_values
        + jnp.minimum(face_speed, 0.0) * right_values
        + diffusion
    )


def interface_ghost(own_face, local_map):
    across = swapped(own_face, "row", 0)
    picked = lax.all_gather(across, "pitch", axis=1, tiled=True)
    return jnp.take(picked, local_map, axis=1)


def update_core(extended, speed_axial, speed_pitch, ghost_face, wall_mask, row_id):
    along_pitch = extended[:, :, 1:-1, :]
    pitch_flux = face_flux(
        along_pitch[:3, :-1],
        along_pitch[:3, 1:],
        along_pitch[3, :-1],
        along_pitch[3, 1:],
        speed_pitch,
    )
    along_radius = extended[:, 1:-1]
    radial_flux = (
        face_flux(
            along_radius[:3, :, :-1],
            along_radius[:3, :, 1:],
            along_radius[3, :, :-1],
            along_radius[3, :, 1:],
            None,
        )
        * wall_mask[:, None]
    )
    core = extended[:, 1:-1, 1:-1]
    pitch_cells = core.shape[1]
    full_stack = jnp.concatenate(
        [core, jnp.broadcast_to(speed_axial[None, None], (1, pitch_cells) + speed_axial.shape)], 0
    )
    upstream = jnp.where(row_id == 0, full_stack[..., 0], ghost_face)
    downstream = jnp.where(row_id == 0, ghost_face, full_stack[..., -1])
    line = jnp.concatenate([upstream[..., None], full_stack, downstream[..., None]], -1)
    face_speed = 0.5 * (line[4, ..., :-1] + line[4, ..., 1:])
    axial_flux = face_flux(
        line[:3, ..., :-1], line[:3, ..., 1:], line[3, ..., :-1], line[3, ..., 1:], face_speed
    )
    divergence = (
        pitch_flux[:, 1:]
        - pitch_flux[:, :-1]
        + radial_flux[:, :, 1:]
        - radial_flux[:, :, :-1]
        + axial_flux[..., 1:]
        - axial_flux[..., :-1]
    )
    return core[:3] - TIME_STEP * divergence


def advance(state, diffusivity, speed_axial, speed_pitch, local_map, wall_mask):
    pitch_cells = state.shape[1]
    stacked = jnp.concatenate([state, diffusivity[None]], 0)
    extended = padded(stacked, (("pitch", 1), ("span", 2)), 1)
    full_stack = jnp.concatenate(
        [stacked, jnp.broadcast_to(speed_axial[None, None], (1, pitch_cells) + speed_axial.shape)],
        0,
    )
    row_id = lax.axis_index("row")
    own_face = jnp.where(row_id == 0, full_stack[..., -1], full_stack[..., 0])
    ghost_face = interface_ghost(own_face, local_map)
    return update_core(extended, speed_axial, speed_pitch, ghost_face, wall_mask, row_id)


def local(
    fields,
    diffusivity,
    mean_flow,
    radial_kernel,
    tracer_values,
    tracer_cells,
    tracer_dest,
    interface_map,
):
    radial_cells = mean_flow.shape[0]
    axial_cells = mean_flow.shape[2]
    flat_width = 2 * axial_cells
    span_id = lax.axis_index("span")
    kernel_cols = lax.dynamic_slice_in_dim(radial_kernel, span_id * radial_cells, radial_cells, 1)
    flat_rows = mean_flow.reshape(radial_cells, flat_width)
    smoothed = lax.psum_scatter(
        jnp.dot(kernel_cols, flat_rows, preferred_element_type=jnp.float32),
        "span",
        scatter_dimension=0,
        tiled=True,
    )
    smoothed = smoothed.reshape(radial_cells, 2, axial_cells)
    speed_axial = AXIAL_SPEED * (1.0 + 0.5 * jnp.tanh(smoothed[:, 0]))
    speed_pitch = PITCH_SPEED * jnp.tanh(smoothed[:, 1])
    plane_size = radial_cells * axial_cells
    sample_fields = jnp.take(fields.reshape(fields.shape[0], -1), tracer_cells, axis=1)
    sample_speed = jnp.take(
        jnp.stack([speed_axial, speed_pitch]).reshape(2, plane_size),
        tracer_cells % plane_size,
        axis=1,
    )
    sampled = jnp.concatenate([sample_fields, sample_speed], 0)
    head_rows = tracer_values[:5]
    tail_rows = tracer_values[5:]
    updated = jnp.concatenate(
        [head_rows + 0.5 * (sampled - head_rows), tail_rows + 0.8 * sampled], 0
    )
    npitch = lax.axis_size("pitch")
    capacity = 2 * tracer_values.shape[1] // npitch
    targets = tracer_dest[:, 0]
    onehot = (targets[:, None] == jnp.arange(npitch, dtype=jnp.int32)[None]).astype(jnp.int32)
    slot_index = jnp.sum((jnp.cumsum(onehot, 0) - onehot) * onehot, 1)
    position = targets * capacity + slot_index
    outgoing = (
        jnp.zeros((tracer_values.shape[0], npitch * capacity), jnp.float32)
        .at[:, position]
        .set(updated)
    )
    arrived = lax.all_to_all(outgoing, "pitch", split_axis=1, concat_axis=1, tiled=True)
    face_index = span_id * radial_cells + jnp.arange(radial_cells + 1, dtype=jnp.int32)
    total_radial = radial_cells * lax.axis_size("span")
    wall_mask = ((face_index > 0) & (face_index < total_radial)).astype(jnp.float32)
    local_map = interface_map[0]
    current = fields
    for substep in range(SUB):
        current = advance(current, diffusivity, speed_axial, speed_pitch, local_map, wall_mask)
    return (current, arrived)


def solution(mesh):
    placed = (
        P(None, "pitch", "span", "row"),
        P("pitch", "span", "row"),
        P("span", None, "row"),
        P(),
        P(None, ("pitch", "span", "row")),
        P(("pitch", "span", "row")),
        P(("pitch", "span", "row"), None),
        P("row", "pitch"),
    )
    return jax.shard_map(
        local,
        mesh=mesh,
        in_specs=placed,
        out_specs=(P(None, "pitch", "span", "row"), P(None, ("pitch", "span", "row"))),
        check_vma=False,
    )
```

profile of v0, /device:TPU:24, one launch (start us, length us, event | category | flops | bytes accessed | tf_op | source)
XLA Modules:
  0.0 287.4 jit_solution(10924218289385498217)
XLA Ops:
  10.5 4.3 %collective-permute-start = (f32[4,1,16,256]{3,2,1,0:T(8,128)}, f32[4,1,16,256]{3,2,1,0:T(8,128)S(1)}, u32[]{:S(2)}, u32[]{:S(2)}) collective-permute-start(f32[4,1,16,256]{3,2,1,0:T(8,128)} %get-tuple-element.57), channel_id=1, source_target_pairs={{0,16},{16,32},{32,48},{48,64},{64,80},{80,96},{96,112},{112,128},... | collective-permute-start | bytes 196616 | tf_op jit(solution)/shard_map/ppermute | solution.py:29
  14.7 10.8 %collective-permute-start.1 = (f32[4,1,16,256]{3,2,1,0:T(8,128)}, f32[4,1,16,256]{3,2,1,0:T(8,128)}, u32[]{:S(2)}, u32[]{:S(2)}) collective-permute-start(f32[4,1,16,256]{3,2,1,0:T(8,128)} %get-tuple-element.58), channel_id=1, source_target_pairs={{16,0},{32,16},{48,32},{64,48},{80,64},{96,80},{112,96},{128,112},... | collective-permute-start | bytes 196616 | tf_op jit(solution)/shard_map/ppermute | solution.py:31
  27.7 16.7 %copy.818 = f32[3,16,16,256]{0,3,2,1:T(8,128)} copy(f32[3,16,16,256]{3,2,1,0:T(8,128)S(1)} %copy-done.2) | data formatting | bytes 1572864 | tf_op args[0]
  44.4 18.2 %gather_fusion = f32[2048,3]{1,0:T(8,128)} fusion(f32[3,65536]{0,1:T(8,128)} %bitcast.121, s32[2048]{0:T(1024)S(1)} %get-tuple-element.74), kind=kCustom, calls=%fused_computation.2 | custom fusion | bytes 57344 | tf_op jit(solution)/shard_map/jit(_take)/gather | solution.py:138
  62.6 2.6 select_bitcast_fusion.1
  65.2 2.2 copy.820
  67.3 9.1 %reduce-window.6 = s32[32,16,128]{2,1,0:T(8,128)S(1)} reduce-window(s32[32,16,128]{2,1,0:T(8,128)S(1)} %fusion.43, s32[]{:T(128)} %constant.30.clone.1), window={size=1x1x128 pad=0_0x0_0x127_0}, to_apply=%region_1.0 | reduce-window | flops 8323072 | bytes 524292 | tf_op jit(solution)/shard_map/reduce-window
  79.0 4.7 %collective-permute-start.2 = (f32[4,18,1,256]{3,0,2,1:T(4,128)S(1)}, f32[4,18,1,256]{3,0,2,1:T(4,128)S(1)}, u32[]{:S(2)}, u32[]{:S(2)}) collective-permute-start(f32[4,18,1,256]{3,0,2,1:T(4,128)S(1)} %copy.846), channel_id=1, source_target_pairs={{0,2},{2,4},{4,6},{6,8},{8,10},{10,12},{12,14},{14,0},{1,3},{3,5},... | collective-permute-start | bytes 221192 | tf_op jit(solution)/shard_map/ppermute | solution.py:29
  85.7 2.2 fusion.14
  98.8 7.6 %gather_fusion.1 = f32[2048,2]{1,0:T(8,128)} fusion(f32[2,4096]{0,1:T(8,128)S(1)} %copy.819, s32[2048]{0:T(1024)S(1)} %get-tuple-element.75), kind=kCustom, calls=%fused_computation.3 | custom fusion | bytes 40960 | tf_op jit(solution)/shard_map/jit(_take)/gather | solution.py:139
  109.8 6.5 %scatter_custom_fusion = f32[10,4096]{0,1:T(8,128)S(1)} fusion(s32[2048]{0:T(1024)} %bitcast.141, f32[2048,10]{1,0:T(8,128)} %copy.822, f32[]{:T(128)} %constant.45.clone.1), kind=kCustom, calls=%fused_computation.51 | custom fusion | bytes 164352 | tf_op jit(solution)/shard_map/scatter | solution.py:159
  117.6 5.2 %all-to-all-start = ((f32[10,32,128]{2,0,1:T(8,128)}), f32[10,32,128]{2,0,1:T(8,128)}, u32[]{:S(2)}, u32[]{:S(2)}) async-start(f32[10,32,128]{2,0,1:T(8,128)} %copy.823), calls=%async_computation.1 | async-start | bytes 524288 | tf_op jit(solution)/shard_map/all_to_all | solution.py:161
  122.8 2.5 fusion.5
  126.2 51.2 %all_gather.6 = f32[5,512,16]{2,1,0:T(8,128)S(1)} all-gather(f32[5,16,16]{2,1,0:T(8,128)S(1)} %copy.782), channel_id=1, replica_groups=mesh['pitch'=32,'span'=8,'row'=2] {'pitch'}, dimensions={1}, use_global_device_ids=true | all-gather | bytes 168960 | tf_op jit(solution)/shard_map/all_gather | solution.py:51
  177.3 2.2 copy.783
  179.5 2.8 gather_fusion.2
  183.9 2.2 copy.786
  198.8 2.7 collective-permute-start.5
  201.4 6.5 %collective-permute-start.6 = (f32[4,1,16,256]{3,2,1,0:T(8,128)S(1)}, f32[4,1,16,256]{3,2,1,0:T(8,128)S(1)}, u32[]{:S(2)}, u32[]{:S(2)}) collective-permute-start(f32[4,1,16,256]{3,2,1,0:T(8,128)S(1)} %get-tuple-element.54), channel_id=1, source_target_pairs={{16,0},{32,16},{48,32},{64,48},{80,64},{96,80},{112,96},{128,112},... | collective-permute-start | bytes 196616 | tf_op jit(solution)/shard_map/ppermute | solution.py:31
  208.0 47.9 %all_gather.7 = f32[5,512,16]{2,1,0:T(8,128)S(1)} all-gather(f32[5,16,16]{2,1,0:T(8,128)S(1)} %copy.807), channel_id=1, replica_groups=mesh['pitch'=32,'span'=8,'row'=2] {'pitch'}, dimensions={1}, use_global_device_ids=true | all-gather | bytes 168960 | tf_op jit(solution)/shard_map/all_gather | solution.py:51
  255.8 2.2 copy.808
  258.0 2.1 gather_fusion.3
  264.8 4.3 %collective-permute-start.7 = (f32[4,18,1,256]{3,0,2,1:T(4,128)S(1)}, f32[4,18,1,256]{3,0,2,1:T(4,128)S(1)}, u32[]{:S(2)}, u32[]{:S(2)}) collective-permute-start(f32[4,18,1,256]{3,0,2,1:T(4,128)S(1)} %copy.851), channel_id=1, source_target_pairs={{0,2},{2,4},{4,6},{6,8},{8,10},{10,12},{12,14},{14,0},{1,3},{3,5},... | collective-permute-start | bytes 221192 | tf_op jit(solution)/shard_map/ppermute | solution.py:29
  273.2 3.3 %collective-permute-done.8 = f32[4,18,1,256]{3,0,2,1:T(4,128)S(1)} collective-permute-done((f32[4,18,1,256]{3,0,2,1:T(4,128)S(1)}, f32[4,18,1,256]{3,0,2,1:T(4,128)S(1)}, u32[]{:S(2)}, u32[]{:S(2)}) %collective-permute-start.8) | collective-permute-done | bytes 73760 | tf_op jit(solution)/shard_map/ppermute | solution.py:31
  (142 shorter events, 52.9 us)
Async XLA Ops:
  7.2 18.4 %copy-start = (bf16[128,128]{1,0:T(8,128)(2,1)S(1)}, bf16[128,128]{1,0:T(8,128)(2,1)}, u32[]{:S(2)}) copy-start(bf16[128,128]{1,0:T(8,128)(2,1)} %param.13) | copy-start | bytes 98308
  7.2 85.3 %reduce-scatter.2.cloned.1.call-start = ((), (), s32[]{:S(2)}) async-start(), calls=%async_computation.2 | async-start | bytes 294912 | tf_op jit(solution)/shard_map/reduce_scatter | solution.py:128
  8.3 17.2 %copy-start.12 = (bf16[16,2,256]{2,1,0:T(2,128)(2,1)S(1)}, bf16[16,2,256]{2,1,0:T(2,128)(2,1)}, u32[]{:S(2)}) copy-start(bf16[16,2,256]{2,1,0:T(2,128)(2,1)} %param.12) | copy-start | bytes 49156
  8.3 18.2 %copy-start.2 = (f32[3,16,16,256]{3,2,1,0:T(8,128)S(1)}, f32[3,16,16,256]{3,2,1,0:T(8,128)}, u32[]{:S(2)}) copy-start(f32[3,16,16,256]{3,2,1,0:T(8,128)} %param.10) | copy-start | bytes 2359300
  9.8 17.2 %copy-start.16 = (s32[1,16]{1,0:T(1,128)S(1)}, s32[1,16]{1,0:T(1,128)}, u32[]{:S(2)}) copy-start(s32[1,16]{1,0:T(1,128)} %param.17) | copy-start | bytes 196
  9.8 17.9 %copy-start.11 = (s32[2048]{0:T(1024)S(1)}, s32[2048]{0:T(1024)}, u32[]{:S(2)}) copy-start(s32[2048]{0:T(1024)} %param.15) | copy-start | bytes 24580
  10.5 67.4 %collective-permute-start = (f32[4,1,16,256]{3,2,1,0:T(8,128)}, f32[4,1,16,256]{3,2,1,0:T(8,128)S(1)}, u32[]{:S(2)}, u32[]{:S(2)}) collective-permute-start(f32[4,1,16,256]{3,2,1,0:T(8,128)} %get-tuple-element.57), channel_id=1, source_target_pairs={{0,16},{16,32},{32,48},{48,64},{64,80},{80,96},{96,112},{112,128},... | collective-permute-start | bytes 196616 | tf_op jit(solution)/shard_map/ppermute | solution.py:29
  14.7 63.1 %collective-permute-start.1 = (f32[4,1,16,256]{3,2,1,0:T(8,128)}, f32[4,1,16,256]{3,2,1,0:T(8,128)}, u32[]{:S(2)}, u32[]{:S(2)}) collective-permute-start(f32[4,1,16,256]{3,2,1,0:T(8,128)} %get-tuple-element.58), channel_id=1, source_target_pairs={{16,0},{32,16},{48,32},{64,48},{80,64},{96,80},{112,96},{128,112},... | collective-permute-start | bytes 196616 | tf_op jit(solution)/shard_map/ppermute | solution.py:31
  27.0 66.3 %copy-start.3 = (f32[3,16,16,256]{3,1,2,0:T(8,128)}, f32[3,16,16,256]{3,1,2,0:T(8,128)S(1)}, u32[]{:S(2)}) copy-start(f32[3,16,16,256]{3,1,2,0:T(8,128)S(1)} %copy.791) | copy-start | bytes 2359300
  62.6 4.7 %copy-start.10 = (s32[2048,1]{0,1:T(1,128)S(1)}, s32[2048,1]{0,1:T(1,128)}, u32[]{:S(2)}) copy-start(s32[2048,1]{0,1:T(1,128)} %param.16) | copy-start | bytes 24580
  77.9 13.4 %copy-start.13 = (f32[17]{0:T(128)}, f32[17]{0:T(128)S(1)}, u32[]{:S(2)}) copy-start(f32[17]{0:T(128)S(1)} %and_convert_fusion) | copy-start | bytes 208
  79.0 10.6 %collective-permute-start.2 = (f32[4,18,1,256]{3,0,2,1:T(4,128)S(1)}, f32[4,18,1,256]{3,0,2,1:T(4,128)S(1)}, u32[]{:S(2)}, u32[]{:S(2)}) collective-permute-start(f32[4,18,1,256]{3,0,2,1:T(4,128)S(1)} %copy.846), channel_id=1, source_target_pairs={{0,2},{2,4},{4,6},{6,8},{8,10},{10,12},{12,14},{14,0},{1,3},{3,5},... | collective-permute-start | bytes 221192 | tf_op jit(solution)/shard_map/ppermute | solution.py:29
  83.7 7.5 %collective-permute-start.3 = (f32[4,18,1,256]{3,0,2,1:T(4,128)S(1)}, f32[4,18,1,256]{3,0,2,1:T(4,128)S(1)}, u32[]{:S(2)}, u32[]{:S(2)}) collective-permute-start(f32[4,18,1,256]{3,0,2,1:T(4,128)S(1)} %copy.847), channel_id=1, source_target_pairs={{2,0},{4,2},{6,4},{8,6},{10,8},{12,10},{14,12},{0,14},{3,1},{5,3},... | collective-permute-start | bytes 221192 | tf_op jit(solution)/shard_map/ppermute | solution.py:31
  96.1 29.2 %collective-permute-start.4 = (f32[5,16,16]{2,0,1:T(8,128)}, f32[5,16,16]{2,0,1:T(8,128)}, u32[]{:S(2)}, u32[]{:S(2)}) collective-permute-start(f32[5,16,16]{2,0,1:T(8,128)} %bitcast_select_fusion.5), channel_id=1, source_target_pairs={{0,1},{1,0},{2,3},{3,2},{4,5},{5,4},{6,7},{7,6},{8,9},{9,8},{10,11... | collective-permute-start | bytes 15368 | tf_op jit(solution)/shard_map/ppermute | solution.py:19
  117.6 161.1 %all-to-all-start = ((f32[10,32,128]{2,0,1:T(8,128)}), f32[10,32,128]{2,0,1:T(8,128)}, u32[]{:S(2)}, u32[]{:S(2)}) async-start(f32[10,32,128]{2,0,1:T(8,128)} %copy.823), calls=%async_computation.1 | async-start | bytes 524288 | tf_op jit(solution)/shard_map/all_to_all | solution.py:161
  177.3 5.0 %copy-start.7 = (f32[5,16,16,1]{2,0,1,3:T(8,128)S(1)}, f32[5,16,16,1]{2,0,1,3:T(8,128)}, u32[]{:S(2)}) copy-start(f32[5,16,16,1]{2,0,1,3:T(8,128)} %copy-done.6) | copy-start | bytes 15364
  177.3 5.0 %copy-start.15 = (pred[16]{0:T(512)(128)(4,1)S(1)}, pred[16]{0:T(512)(128)(4,1)}, u32[]{:S(2)}) copy-start(pred[16]{0:T(512)(128)(4,1)} %compare_and_fusion.2) | copy-start | bytes 52
  179.5 8.0 %copy-start.4 = (f32[3,16,16,256]{3,1,2,0:T(8,128)S(1)}, f32[3,16,16,256]{3,1,2,0:T(8,128)}, u32[]{:S(2)}) copy-start(f32[3,16,16,256]{3,1,2,0:T(8,128)} %copy-done.3) | copy-start | bytes 2359300
  196.2 11.7 %collective-permute-start.9 = (f32[5,16,16]{2,0,1:T(8,128)S(1)}, f32[5,16,16]{2,0,1:T(8,128)S(1)}, u32[]{:S(2)}, u32[]{:S(2)}) collective-permute-start(f32[5,16,16]{2,0,1:T(8,128)S(1)} %bitcast_select_fusion.2), channel_id=1, source_target_pairs={{0,1},{1,0},{2,3},{3,2},{4,5},{5,4},{6,7},{7,6},{8,9},{9,8},{10,11... | collective-permute-start | bytes 15368 | tf_op jit(solution)/shard_map/ppermute | solution.py:19
  198.8 65.5 %collective-permute-start.5 = (f32[4,1,16,256]{3,2,1,0:T(8,128)}, f32[4,1,16,256]{3,2,1,0:T(8,128)S(1)}, u32[]{:S(2)}, u32[]{:S(2)}) collective-permute-start(f32[4,1,16,256]{3,2,1,0:T(8,128)} %get-tuple-element.53), channel_id=1, source_target_pairs={{0,16},{16,32},{32,48},{48,64},{64,80},{80,96},{96,112},{112,128},... | collective-permute-start | bytes 196616 | tf_op jit(solution)/shard_map/ppermute | solution.py:29
  201.4 62.9 %collective-permute-start.6 = (f32[4,1,16,256]{3,2,1,0:T(8,128)S(1)}, f32[4,1,16,256]{3,2,1,0:T(8,128)S(1)}, u32[]{:S(2)}, u32[]{:S(2)}) collective-permute-start(f32[4,1,16,256]{3,2,1,0:T(8,128)S(1)} %get-tuple-element.54), channel_id=1, source_target_pairs={{16,0},{32,16},{48,32},{64,48},{80,64},{96,80},{112,96},{128,112},... | collective-permute-start | bytes 196616 | tf_op jit(solution)/shard_map/ppermute | solution.py:31
  264.8 7.7 %collective-permute-start.7 = (f32[4,18,1,256]{3,0,2,1:T(4,128)S(1)}, f32[4,18,1,256]{3,0,2,1:T(4,128)S(1)}, u32[]{:S(2)}, u32[]{:S(2)}) collective-permute-start(f32[4,18,1,256]{3,0,2,1:T(4,128)S(1)} %copy.851), channel_id=1, source_target_pairs={{0,2},{2,4},{4,6},{6,8},{8,10},{10,12},{12,14},{14,0},{1,3},{3,5},... | collective-permute-start | bytes 221192 | tf_op jit(solution)/shard_map/ppermute | solution.py:29
  269.0 7.5 %collective-permute-start.8 = (f32[4,18,1,256]{3,0,2,1:T(4,128)S(1)}, f32[4,18,1,256]{3,0,2,1:T(4,128)S(1)}, u32[]{:S(2)}, u32[]{:S(2)}) collective-permute-start(f32[4,18,1,256]{3,0,2,1:T(4,128)S(1)} %copy.852), channel_id=1, source_target_pairs={{2,0},{4,2},{6,4},{8,6},{10,8},{12,10},{14,12},{0,14},{3,1},{5,3},... | collective-permute-start | bytes 221192 | tf_op jit(solution)/shard_map/ppermute | solution.py:31
  272.4 4.2 %copy-start.14 = (f32[17]{0:T(128)S(1)}, f32[17]{0:T(128)}, u32[]{:S(2)}) copy-start(f32[17]{0:T(128)} %copy-done.13) | copy-start | bytes 208
  (5 other events, 11.4 us)
Sparse Core Ops, SparseCore 0:
  26.7 35.2 reduce-scatter.1
where the time goes:
time: 289 us; the launch traced here: 287 us
  blocking collectives  99 us (34%)
  local copies, waits for them, and re-layouts  89.4 us (31%)
  starting transfers between devices  46.3 us (16%)
  other arithmetic  32.7 us (11%)
  between operations  14.8 us (5%)
  waiting for transfers between devices  4.27 us (1%)
    all_gather x2, blocking collectives, interface_ghost(): picked = lax.all_gather(across, 'pitch', axis=1, tiled=True)  99 us
    unnamed x53, local copies, waits for them, and re-layouts  24.7 us
    ppermute x4, starting transfers between devices, padded(): lax.ppermute(head, axis, [((i + 1) % count, i) for i in range(count)])  21.3 us
    gather x1, local copies, waits for them, and re-layouts, local(): jnp.take(fields.reshape(fields.shape[0], -1), tracer_cells, axis=1)  18.2 us
    ppermute x4, starting transfers between devices, padded(): lax.ppermute(tail, axis, [(i, (i + 1) % count) for i in range(count)])  15.9 us
    another operation x3, other arithmetic  9.41 us
    gather x1, local copies, waits for them, and re-layouts, local(): jnp.take(jnp.stack([speed_axial, speed_pitch]).reshape(2, plane_size), tr...  7.6 us
    scatter x1, local copies, waits for them, and re-layouts, local(): outgoing = jnp.zeros((tracer_values.shape[0], npitch * capacity), jnp.flo...  6.46 us
  transfers between devices with their start and end apart: 12, of which 2 were waited for; matrix products, arithmetic and copies ran while one was open for 39% of the time, Pallas kernels for 0%

commit v1 on v0

--- a/solution.py
+++ b/solution.py
@@ -158,7 +158,12 @@
         .at[:, position]
         .set(updated)
     )
-    arrived = lax.all_to_all(outgoing, "pitch", split_axis=1, concat_axis=1, tiled=True)
+    arrived = jnp.concatenate(
+        lax.all_to_all(
+            jnp.stack(jnp.split(outgoing, lax.axis_size("pitch"), axis=1)), "pitch", 0, 0
+        ),
+        axis=1,
+    )
     face_index = span_id * radial_cells + jnp.arange(radial_cells + 1, dtype=jnp.int32)
     total_radial = radial_cells * lax.axis_size("span")
     wall_mask = ((face_index > 0) & (face_index < total_radial)).astype(jnp.float32)

time: 289 us -> 307 us (1.062)
  local copies, waits for them, and re-layouts: 89.4 us -> 111 us
    unnamed x53 -> x86, local copies, waits for them, and re-layouts: 24.7 us -> 46.4 us
    another operation x1 -> x3, local copies, waits for them, and re-layouts: 0.24 us -> 3.78 us  [the longest x2 3.54 us: local(): jnp.stack(jnp.split(outgoing, lax.axis_size('pitch'), axis=1))]
  transfers between devices with their start and end apart: 12 -> 12, of which waited for: 2 -> 2; matrix products, arithmetic and copies ran while one was open for 39% -> 31% of each run, Pallas kernels for 0% -> 0%
where the time goes in v1:
time: 307 us; the launch traced here: 306 us
  local copies, waits for them, and re-layouts  111 us (36%)
  blocking collectives  99.1 us (32%)
  starting transfers between devices  45.9 us (15%)
  other arithmetic  30 us (10%)
  between operations  14.8 us (5%)
  waiting for transfers between devices  3.86 us (1%)
    all_gather x2, blocking collectives, interface_ghost(): picked = lax.all_gather(across, 'pitch', axis=1, tiled=True)  99.1 us
    unnamed x86, local copies, waits for them, and re-layouts  46.4 us
    ppermute x4, starting transfers between devices, padded(): lax.ppermute(head, axis, [((i + 1) % count, i) for i in range(count)])  22.4 us
    gather x1, local copies, waits for them, and re-layouts, local(): jnp.take(fields.reshape(fields.shape[0], -1), tracer_cells, axis=1)  18.2 us
    ppermute x4, starting transfers between devices, padded(): lax.ppermute(tail, axis, [(i, (i + 1) % count) for i in range(count)])  14.4 us
    another operation x3, other arithmetic  9.41 us
    gather x1, local copies, waits for them, and re-layouts, local(): jnp.take(jnp.stack([speed_axial, speed_pitch]).reshape(2, plane_size), tr...  7.6 us
    scatter x1, local copies, waits for them, and re-layouts, local(): outgoing = jnp.zeros((tracer_values.shape[0], npitch * capacity), jnp.flo...  6.46 us
  transfers between devices with their start and end apart: 12, of which 2 were waited for; matrix products, arithmetic and copies ran while one was open for 31% of the time, Pallas kernels for 0%

profile of v1, /device:TPU:24, one launch (start us, length us, event | category | flops | bytes accessed | tf_op | source)
XLA Modules:
  0.0 306.1 jit_solution(11647644536798762589)
XLA Ops:
  11.5 4.3 %collective-permute-start = (f32[4,1,16,256]{3,2,1,0:T(8,128)S(1)}, f32[4,1,16,256]{3,2,1,0:T(8,128)S(1)}, u32[]{:S(2)}, u32[]{:S(2)}) collective-permute-start(f32[4,1,16,256]{3,2,1,0:T(8,128)S(1)} %get-tuple-element.59), channel_id=1, source_target_pairs={{0,16},{16,32},{32,48},{48,64},{64,80},{80,96},{96,112},{112,128},... | collective-permute-start | bytes 196616 | tf_op jit(solution)/shard_map/ppermute | solution.py:29
  15.8 10.8 %collective-permute-start.1 = (f32[4,1,16,256]{3,2,1,0:T(8,128)S(1)}, f32[4,1,16,256]{3,2,1,0:T(8,128)S(1)}, u32[]{:S(2)}, u32[]{:S(2)}) collective-permute-start(f32[4,1,16,256]{3,2,1,0:T(8,128)S(1)} %get-tuple-element.60), channel_id=1, source_target_pairs={{16,0},{32,16},{48,32},{64,48},{80,64},{96,80},{112,96},{128,112},... | collective-permute-start | bytes 196616 | tf_op jit(solution)/shard_map/ppermute | solution.py:31
  26.6 16.7 %copy.882 = f32[3,16,16,256]{0,3,2,1:T(8,128)} copy(f32[3,16,16,256]{3,2,1,0:T(8,128)S(1)} %copy-done.2) | data formatting | bytes 1572864 | tf_op args[0]
  45.2 18.2 %gather_fusion = f32[2048,3]{1,0:T(8,128)} fusion(f32[3,65536]{0,1:T(8,128)} %bitcast.249, s32[2048]{0:T(1024)S(1)} %get-tuple-element.76), kind=kCustom, calls=%fused_computation.2 | custom fusion | bytes 57344 | tf_op jit(solution)/shard_map/jit(_take)/gather | solution.py:138
  65.4 9.1 %reduce-window.6 = s32[32,16,128]{2,1,0:T(8,128)S(1)} reduce-window(s32[32,16,128]{2,1,0:T(8,128)S(1)} %fusion.43, s32[]{:T(128)} %constant.30.clone.1), window={size=1x1x128 pad=0_0x0_0x127_0}, to_apply=%region_1.0 | reduce-window | flops 8323072 | bytes 524292 | tf_op jit(solution)/shard_map/reduce-window
  76.2 4.7 %collective-permute-start.2 = (f32[4,18,1,256]{3,0,2,1:T(4,128)S(1)}, f32[4,18,1,256]{3,0,2,1:T(4,128)S(1)}, u32[]{:S(2)}, u32[]{:S(2)}) collective-permute-start(f32[4,18,1,256]{3,0,2,1:T(4,128)S(1)} %copy.910), channel_id=1, source_target_pairs={{0,2},{2,4},{4,6},{6,8},{8,10},{10,12},{12,14},{14,0},{1,3},{3,5},... | collective-permute-start | bytes 221192 | tf_op jit(solution)/shard_map/ppermute | solution.py:29
  85.9 2.4 collective-permute-done.3
  91.2 7.6 %gather_fusion.1 = f32[2048,2]{1,0:T(8,128)} fusion(f32[2,4096]{0,1:T(8,128)S(1)} %copy.883, s32[2048]{0:T(1024)S(1)} %get-tuple-element.77), kind=kCustom, calls=%fused_computation.3 | custom fusion | bytes 40960 | tf_op jit(solution)/shard_map/jit(_take)/gather | solution.py:139
  102.2 6.5 %scatter_custom_fusion = f32[10,4096]{0,1:T(8,128)S(1)} fusion(s32[2048]{0:T(1024)} %bitcast.269, f32[2048,10]{1,0:T(8,128)} %copy.886, f32[]{:T(128)} %constant.45.clone.1), kind=kCustom, calls=%fused_computation.51 | custom fusion | bytes 164352 | tf_op jit(solution)/shard_map/scatter | solution.py:159
  128.6 2.9 copy.887
  131.5 5.1 %all-to-all-start = ((f32[32,10,128]{2,1,0:T(8,128)}), f32[32,10,128]{2,1,0:T(8,128)S(1)}, u32[]{:S(2)}, u32[]{:S(2)}) async-start(f32[32,10,128]{2,1,0:T(8,128)} %copy.887), calls=%async_computation.1 | async-start | bytes 524288 | tf_op jit(solution)/shard_map/all_to_all | solution.py:162
  145.1 3.0 fusion.5
  148.1 51.2 %all_gather.6 = f32[5,512,16]{2,1,0:T(8,128)S(1)} all-gather(f32[5,16,16]{2,1,0:T(8,128)S(1)} %copy.846), channel_id=1, replica_groups=mesh['pitch'=32,'span'=8,'row'=2] {'pitch'}, dimensions={1}, use_global_device_ids=true | all-gather | bytes 168960 | tf_op jit(solution)/shard_map/all_gather | solution.py:51
  199.3 2.2 copy.847
  201.5 2.1 gather_fusion.2
  214.6 1.9 collective-permute-start.9
  217.2 2.7 collective-permute-start.5
  219.9 6.4 %collective-permute-start.6 = (f32[4,1,16,256]{3,2,1,0:T(8,128)}, f32[4,1,16,256]{3,2,1,0:T(8,128)S(1)}, u32[]{:S(2)}, u32[]{:S(2)}) collective-permute-start(f32[4,1,16,256]{3,2,1,0:T(8,128)} %get-tuple-element.56), channel_id=1, source_target_pairs={{16,0},{32,16},{48,32},{64,48},{80,64},{96,80},{112,96},{128,112},... | collective-permute-start | bytes 196616 | tf_op jit(solution)/shard_map/ppermute | solution.py:31
  226.4 47.9 %all_gather.7 = f32[5,512,16]{2,1,0:T(8,128)S(1)} all-gather(f32[5,16,16]{2,1,0:T(8,128)S(1)} %copy.871), channel_id=1, replica_groups=mesh['pitch'=32,'span'=8,'row'=2] {'pitch'}, dimensions={1}, use_global_device_ids=true | all-gather | bytes 168960 | tf_op jit(solution)/shard_map/all_gather | solution.py:51
  274.2 2.2 copy.872
  276.4 2.1 gather_fusion.3
  280.7 2.2 copy.878
  285.8 2.8 collective-permute-start.7
  288.6 3.3 %collective-permute-start.8 = (f32[4,18,1,256]{3,0,2,1:T(4,128)S(1)}, f32[4,18,1,256]{3,0,2,1:T(4,128)S(1)}, u32[]{:S(2)}, u32[]{:S(2)}) collective-permute-start(f32[4,18,1,256]{3,0,2,1:T(4,128)S(1)} %copy.916), channel_id=1, source_target_pairs={{2,0},{4,2},{6,4},{8,6},{10,8},{12,10},{14,12},{0,14},{3,1},{5,3},... | collective-permute-start | bytes 221192 | tf_op jit(solution)/shard_map/ppermute | solution.py:31
  (176 shorter events, 73.0 us)
Async XLA Ops:
  7.2 19.4 %copy-start.2 = (f32[3,16,16,256]{3,2,1,0:T(8,128)S(1)}, f32[3,16,16,256]{3,2,1,0:T(8,128)}, u32[]{:S(2)}) copy-start(f32[3,16,16,256]{3,2,1,0:T(8,128)} %param.10) | copy-start | bytes 2359300
  7.2 19.4 %copy-start.13 = (s32[2048]{0:T(1024)S(1)}, s32[2048]{0:T(1024)}, u32[]{:S(2)}) copy-start(s32[2048]{0:T(1024)} %param.15) | copy-start | bytes 24580
  7.2 82.4 %reduce-scatter.2.cloned.1.call-start = ((), (), s32[]{:S(2)}) async-start(), calls=%async_computation.2 | async-start | bytes 294912 | tf_op jit(solution)/shard_map/reduce_scatter | solution.py:128
  11.5 64.4 %collective-permute-start = (f32[4,1,16,256]{3,2,1,0:T(8,128)S(1)}, f32[4,1,16,256]{3,2,1,0:T(8,128)S(1)}, u32[]{:S(2)}, u32[]{:S(2)}) collective-permute-start(f32[4,1,16,256]{3,2,1,0:T(8,128)S(1)} %get-tuple-element.59), channel_id=1, source_target_pairs={{0,16},{16,32},{32,48},{48,64},{64,80},{80,96},{96,112},{112,128},... | collective-permute-start | bytes 196616 | tf_op jit(solution)/shard_map/ppermute | solution.py:29
  15.8 60.1 %collective-permute-start.1 = (f32[4,1,16,256]{3,2,1,0:T(8,128)S(1)}, f32[4,1,16,256]{3,2,1,0:T(8,128)S(1)}, u32[]{:S(2)}, u32[]{:S(2)}) collective-permute-start(f32[4,1,16,256]{3,2,1,0:T(8,128)S(1)} %get-tuple-element.60), channel_id=1, source_target_pairs={{16,0},{32,16},{48,32},{64,48},{80,64},{96,80},{112,96},{128,112},... | collective-permute-start | bytes 196616 | tf_op jit(solution)/shard_map/ppermute | solution.py:31
  26.6 18.1 %copy-start.17 = (s32[1,16]{1,0:T(1,128)S(1)}, s32[1,16]{1,0:T(1,128)}, u32[]{:S(2)}) copy-start(s32[1,16]{1,0:T(1,128)} %param.17) | copy-start | bytes 196
  44.7 20.6 %copy-start.12 = (s32[2048,1]{0,1:T(1,128)S(1)}, s32[2048,1]{0,1:T(1,128)}, u32[]{:S(2)}) copy-start(s32[2048,1]{0,1:T(1,128)} %param.16) | copy-start | bytes 24580
  75.9 12.5 %copy-start.14 = (f32[17]{0:T(128)}, f32[17]{0:T(128)S(1)}, u32[]{:S(2)}) copy-start(f32[17]{0:T(128)S(1)} %and_convert_fusion) | copy-start | bytes 208
  76.2 9.0 %collective-permute-start.2 = (f32[4,18,1,256]{3,0,2,1:T(4,128)S(1)}, f32[4,18,1,256]{3,0,2,1:T(4,128)S(1)}, u32[]{:S(2)}, u32[]{:S(2)}) collective-permute-start(f32[4,18,1,256]{3,0,2,1:T(4,128)S(1)} %copy.910), channel_id=1, source_target_pairs={{0,2},{2,4},{4,6},{6,8},{8,10},{10,12},{12,14},{14,0},{1,3},{3,5},... | collective-permute-start | bytes 221192 | tf_op jit(solution)/shard_map/ppermute | solution.py:29
  80.9 7.5 %collective-permute-start.3 = (f32[4,18,1,256]{3,0,2,1:T(4,128)S(1)}, f32[4,18,1,256]{3,0,2,1:T(4,128)S(1)}, u32[]{:S(2)}, u32[]{:S(2)}) collective-permute-start(f32[4,18,1,256]{3,0,2,1:T(4,128)S(1)} %copy.911), channel_id=1, source_target_pairs={{2,0},{4,2},{6,4},{8,6},{10,8},{12,10},{14,12},{0,14},{3,1},{5,3},... | collective-permute-start | bytes 221192 | tf_op jit(solution)/shard_map/ppermute | solution.py:31
  91.2 9.5 %copy-start.11 = (f32[10,2048]{1,0:T(8,128)S(1)}, f32[10,2048]{1,0:T(8,128)}, u32[]{:S(2)}) copy-start(f32[10,2048]{1,0:T(8,128)} %param.14) | copy-start | bytes 245764
  131.5 166.8 %all-to-all-start = ((f32[32,10,128]{2,1,0:T(8,128)}), f32[32,10,128]{2,1,0:T(8,128)S(1)}, u32[]{:S(2)}, u32[]{:S(2)}) async-start(f32[32,10,128]{2,1,0:T(8,128)} %copy.887), calls=%async_computation.1 | async-start | bytes 524288 | tf_op jit(solution)/shard_map/all_to_all | solution.py:162
  138.0 7.1 %copy-start.6 = (f32[3,17,16,256]{3,2,1,0:T(8,128)S(1)}, f32[3,17,16,256]{3,2,1,0:T(8,128)}, u32[]{:S(2)}) copy-start(f32[3,17,16,256]{3,2,1,0:T(8,128)} %get-tuple-element.57) | copy-start | bytes 2506756
  138.0 7.1 %copy-start.7 = (f32[3,17,16,256]{3,2,1,0:T(8,128)S(1)}, f32[3,17,16,256]{3,2,1,0:T(8,128)}, u32[]{:S(2)}) copy-start(f32[3,17,16,256]{3,2,1,0:T(8,128)} %get-tuple-element.58) | copy-start | bytes 2506756
  143.1 5.0 %collective-permute-start.4 = (f32[5,16,16]{2,0,1:T(8,128)S(1)}, f32[5,16,16]{2,0,1:T(8,128)S(1)}, u32[]{:S(2)}, u32[]{:S(2)}) collective-permute-start(f32[5,16,16]{2,0,1:T(8,128)S(1)} %bitcast_select_fusion.5), channel_id=1, source_target_pairs={{0,1},{1,0},{2,3},{3,2},{4,5},{5,4},{6,7},{7,6},{8,9},{9,8},{10,11... | collective-permute-start | bytes 15368 | tf_op jit(solution)/shard_map/ppermute | solution.py:19
  199.3 4.3 %copy-start.16 = (pred[16]{0:T(512)(128)(4,1)S(1)}, pred[16]{0:T(512)(128)(4,1)}, u32[]{:S(2)}) copy-start(pred[16]{0:T(512)(128)(4,1)} %compare_and_fusion.2) | copy-start | bytes 52
  199.3 6.4 %copy-start.3 = (f32[3,16,16,256]{3,1,2,0:T(8,128)S(1)}, f32[3,16,16,256]{3,1,2,0:T(8,128)}, u32[]{:S(2)}) copy-start(f32[3,16,16,256]{3,1,2,0:T(8,128)} %copy.855) | copy-start | bytes 2359300
  214.5 5.4 %copy-start.9 = (f32[5,16,16,1]{2,0,1,3:T(8,128)}, f32[5,16,16,1]{2,0,1,3:T(8,128)S(1)}, u32[]{:S(2)}) copy-start(f32[5,16,16,1]{2,0,1,3:T(8,128)S(1)} %copy.899) | copy-start | bytes 15364
  214.6 11.8 %collective-permute-start.9 = (f32[5,16,16]{2,0,1:T(8,128)S(1)}, f32[5,16,16]{2,0,1:T(8,128)S(1)}, u32[]{:S(2)}, u32[]{:S(2)}) collective-permute-start(f32[5,16,16]{2,0,1:T(8,128)S(1)} %bitcast_select_fusion.2), channel_id=1, source_target_pairs={{0,1},{1,0},{2,3},{3,2},{4,5},{5,4},{6,7},{7,6},{8,9},{9,8},{10,11... | collective-permute-start | bytes 15368 | tf_op jit(solution)/shard_map/ppermute | solution.py:19
  217.2 67.9 %collective-permute-start.5 = (f32[4,1,16,256]{3,2,1,0:T(8,128)}, f32[4,1,16,256]{3,2,1,0:T(8,128)S(1)}, u32[]{:S(2)}, u32[]{:S(2)}) collective-permute-start(f32[4,1,16,256]{3,2,1,0:T(8,128)} %get-tuple-element.55), channel_id=1, source_target_pairs={{0,16},{16,32},{32,48},{48,64},{64,80},{80,96},{96,112},{112,128},... | collective-permute-start | bytes 196616 | tf_op jit(solution)/shard_map/ppermute | solution.py:29
  219.9 65.1 %collective-permute-start.6 = (f32[4,1,16,256]{3,2,1,0:T(8,128)}, f32[4,1,16,256]{3,2,1,0:T(8,128)S(1)}, u32[]{:S(2)}, u32[]{:S(2)}) collective-permute-start(f32[4,1,16,256]{3,2,1,0:T(8,128)} %get-tuple-element.56), channel_id=1, source_target_pairs={{16,0},{32,16},{48,32},{64,48},{80,64},{96,80},{112,96},{128,112},... | collective-permute-start | bytes 196616 | tf_op jit(solution)/shard_map/ppermute | solution.py:31
  274.2 4.3 %copy-start.10 = (f32[5,16,16,1]{2,0,1,3:T(8,128)S(1)}, f32[5,16,16,1]{2,0,1,3:T(8,128)}, u32[]{:S(2)}) copy-start(f32[5,16,16,1]{2,0,1,3:T(8,128)} %copy-done.9) | copy-start | bytes 15364
  285.8 8.1 %collective-permute-start.7 = (f32[4,18,1,256]{3,0,2,1:T(4,128)S(1)}, f32[4,18,1,256]{3,0,2,1:T(4,128)S(1)}, u32[]{:S(2)}, u32[]{:S(2)}) collective-permute-start(f32[4,18,1,256]{3,0,2,1:T(4,128)S(1)} %copy.915), channel_id=1, source_target_pairs={{0,2},{2,4},{4,6},{6,8},{8,10},{10,12},{12,14},{14,0},{1,3},{3,5},... | collective-permute-start | bytes 221192 | tf_op jit(solution)/shard_map/ppermute | solution.py:29
  288.6 7.5 %collective-permute-start.8 = (f32[4,18,1,256]{3,0,2,1:T(4,128)S(1)}, f32[4,18,1,256]{3,0,2,1:T(4,128)S(1)}, u32[]{:S(2)}, u32[]{:S(2)}) collective-permute-start(f32[4,18,1,256]{3,0,2,1:T(4,128)S(1)} %copy.916), channel_id=1, source_target_pairs={{2,0},{4,2},{6,4},{8,6},{10,8},{12,10},{14,12},{0,14},{3,1},{5,3},... | collective-permute-start | bytes 221192 | tf_op jit(solution)/shard_map/ppermute | solution.py:31
  (6 other events, 9.2 us)
Sparse Core Ops, SparseCore 0:
  11.4 43.3 reduce-scatter.1
